TPU v7x, 32 devices: a whole 2x2x4 slice. The times are simulated.
32 devices in a mesh: req: 8 (over z, x), mlp: 4 (over y, core).
Axes of the slice: x: 2, y: 2, z: 4, core: 2. Of those that a mesh axis runs over, the one named last changes fastest.
Arguments:
- tokens: bfloat16 [8192, 2048], P('req'), may hold values from -6 to 6
- first_gain: float32 [2048], replicated, may hold values from 0.5 to 1.5
- joined_weight: bfloat16 [2048, 6144], P(None, 'mlp'), may hold values from -0.125 to 0.125
- dense_weight: bfloat16 [2048, 2048], P('mlp'), may hold values from -0.125 to 0.125
- adapter_down: bfloat16 [64, 16, 2048], P('req', None, 'mlp'), may hold values from -0.125 to 0.125
- adapter_up: bfloat16 [64, 16, 2048], P('req'), may hold values from -1.5 to 1.5
- adapter_ids: int32 [64], replicated, may hold values from 0 to 63, as said below
- adapter_rows: int32 [64], replicated, may hold values from 0 to 63, each once
- second_gain: float32 [2048], replicated, may hold values from 0.5 to 1.5
- up_weight: bfloat16 [2048, 8192], P(None, 'mlp'), may hold values from -0.125 to 0.125
- down_weight: bfloat16 [8192, 2048], P('mlp'), may hold values from -0.0625 to 0.0625
- page_pool: bfloat16 [96, 128, 4096], P('req', None, 'mlp'), may hold values from -100 to 100
- page_table: int32 [16, 4], P('req'), may hold values from 0 to 11, as said below
- group_index: int32 [64], P('req'), may hold values from 0 to 1
- lengths: int32 [64], P('req'), may hold values from 1 to 128, as said below
- migrants: int32 [32], P('req'), may hold values from 0 to 7, as said below
- landing: int32 [32], replicated, may hold values from 0 to 63, as said below
Outputs:
- layer_out: bfloat16 [8192, 2048], P(('req', 'mlp'))
- page_out: bfloat16 [64, 128, 4096], P('req', None, 'mlp')
Inputs may be any that keep to these rules, and one draw needn't show every extreme that they name: `adapter_ids`: the requests name exactly 16 distinct adapters in all. `lengths`: each request owner holds at least one request of 128 tokens. `page_table`: the 8 entries of one owner's rows are distinct. `migrants`: entries m // 4 = o name 4 distinct requests of owner o. `landing`: A rearrangement of the slots (m // 4) * 8 + migrants[m] of all migrating requests; the 4 requests of one owner land on 4 distinct other owners, and every owner receives exactly 4 of them.
All inputs are finite; a program needn't handle non-finite values.
Results may differ from a plain program's by a relative error of at most 0.013.
The roundings to bfloat16 on the way count: a program that leaves them out, or rounds other values in their place, can miss the bound.
Values may be sent and summed in bfloat16 or wider, within the bound.
A program may use at most 192 MiB of HBM per device.

v0:
```python
import math
import jax
import jax.numpy as jnp
from jax import lax
from jax.sharding import PartitionSpec as P

HEADS = 16
HD = 128
ADAPTERS = 64
EPS = 1e-05


def layer_norm(values, gain):
    values = values.astype(jnp.float32)
    mean = jnp.mean(values, axis=-1, keepdims=True)
    centred = values - mean
    variance = jnp.mean(centred * centred, axis=-1, keepdims=True)
    return (centred * lax.rsqrt(variance + EPS) * gain).astype(jnp.bfloat16)


def gelu_tanh(value):
    return 0.5 * value * (1.0 + jnp.tanh(0.7978845608 * (value + 0.044715 * value * value * value)))


def attend(queries, keys, values, prefix_keys, prefix_values, lens, slopes):
    scale = 1.0 / math.sqrt(queries.shape[-1])
    own_len = queries.shape[1]
    pre_len = prefix_keys.shape[1]
    s_pre = (
        jnp.einsum("rihe,rphe->rhip", queries, prefix_keys, preferred_element_type=jnp.float32)
        * scale
    )
    s_own = jnp.einsum("rihe,rjhe->rhij", queries, keys, preferred_element_type=jnp.float32) * scale
    own_pos = jnp.arange(own_len).astype(jnp.float32)
    pre_pos = jnp.arange(pre_len).astype(jnp.float32)
    s_pre = (
        s_pre
        - slopes[None, :, None, None]
        * ((pre_len + own_pos)[:, None] - pre_pos[None, :])[None, None]
    )
    s_own = s_own - slopes[None, :, None, None] * (own_pos[:, None] - own_pos[None, :])[None, None]
    steps = jnp.arange(own_len, dtype=jnp.int32)
    allowed = (steps[None, :] <= steps[:, None])[None, None] & (
        steps[None, None, None, :] < lens[:, None, None, None]
    )
    s_own = jnp.where(allowed, s_own, -jnp.inf)
    top = jnp.maximum(jnp.max(s_pre, axis=-1), jnp.max(s_own, axis=-1))[..., None]
    e_pre = jnp.exp(s_pre - top)
    e_own = jnp.exp(s_own - top)
    total = jnp.sum(e_pre, axis=-1, keepdims=True) + jnp.sum(e_own, axis=-1, keepdims=True)
    w_pre = (e_pre / total).astype(jnp.bfloat16)
    w_own = (e_own / total).astype(jnp.bfloat16)
    mixed = jnp.einsum("rhip,rphe->rihe", w_pre, prefix_values, preferred_element_type=jnp.float32)
    mixed = mixed + jnp.einsum("rhij,rjhe->rihe", w_own, values, preferred_element_type=jnp.float32)
    return mixed.astype(jnp.bfloat16)


def shards(
    tokens,
    first_gain,
    joined_weight,
    dense_weight,
    adapter_down,
    adapter_up,
    adapter_ids,
    adapter_rows,
    second_gain,
    up_weight,
    down_weight,
    page_pool,
    page_table,
    group_index,
    lengths,
    migrants,
    landing,
):
    mlp_count = lax.axis_size("mlp")
    req_index = lax.axis_index("req")
    mlp_index = lax.axis_index("mlp")
    requests = lengths.shape[0]
    slot = tokens.shape[0] // requests
    local_heads = joined_weight.shape[1] // (3 * HD)
    row_share = tokens.shape[0] // mlp_count
    own_requests = requests // mlp_count
    normed = layer_norm(tokens, first_gain)
    joined = jnp.dot(normed, joined_weight, preferred_element_type=jnp.float32).astype(jnp.bfloat16)
    joined = joined.reshape(requests, slot, local_heads, 3, HD)
    valid = jnp.arange(slot, dtype=jnp.int32)[None, :] < lengths[:, None]
    fresh = joined[:, :, :, 1:, :].reshape(requests, slot, local_heads * 2 * HD)
    fresh = jnp.where(valid[:, :, None], fresh, jnp.zeros((), jnp.bfloat16))
    pages = page_table[group_index]
    pool_view = page_pool.reshape(page_pool.shape[0], page_pool.shape[1], local_heads, 2, HD)
    prefix = pool_view[pages].reshape(
        requests, pages.shape[1] * page_pool.shape[1], local_heads, 2, HD
    )
    head_pos = (mlp_index * local_heads + jnp.arange(local_heads, dtype=jnp.int32)).astype(
        jnp.float32
    )
    slopes = jnp.exp2(-8.0 * (head_pos + 1.0) / HEADS)
    attended = attend(
        joined[:, :, :, 0],
        joined[:, :, :, 1],
        joined[:, :, :, 2],
        prefix[:, :, :, 0],
        prefix[:, :, :, 1],
        lengths,
        slopes,
    )
    attended_req = attended.reshape(requests, slot, local_heads * HD)
    local_ids = lax.dynamic_slice_in_dim(adapter_ids, req_index * requests, requests)
    every_down, every_up = (
        lax.all_gather(adapter_down, "req", axis=0, tiled=True),
        lax.all_gather(adapter_up, "req", axis=0, tiled=True),
    )
    table_rows = adapter_rows[local_ids]
    pick = (table_rows[:, None] == jnp.arange(ADAPTERS, dtype=jnp.int32)[None, :]).astype(
        jnp.bfloat16
    )
    chosen_down = jnp.einsum(
        "ra,akd->rkd", pick, every_down, preferred_element_type=jnp.float32
    ).astype(jnp.bfloat16)
    chosen_up = jnp.einsum(
        "ra,akd->rkd", pick, every_up, preferred_element_type=jnp.float32
    ).astype(jnp.bfloat16)
    dense_part = jnp.dot(
        attended.reshape(requests * slot, local_heads * HD),
        dense_weight,
        preferred_element_type=jnp.float32,
    )
    low_part = jnp.einsum(
        "rsd,rkd->rsk", attended_req, chosen_down, preferred_element_type=jnp.float32
    )
    low_part = low_part.reshape(requests * slot, low_part.shape[2])
    dense, low = (
        lax.psum_scatter(
            dense_part.astype(jnp.bfloat16), "mlp", scatter_dimension=0, tiled=True
        ).astype(jnp.float32),
        lax.psum_scatter(
            low_part.astype(jnp.bfloat16), "mlp", scatter_dimension=0, tiled=True
        ).astype(jnp.float32),
    )
    low = low.astype(jnp.bfloat16).reshape(own_requests, slot, low.shape[1])
    own_up = lax.dynamic_slice_in_dim(chosen_up, mlp_index * own_requests, own_requests)
    delta = jnp.einsum("rsk,rkd->rsd", low, own_up, preferred_element_type=jnp.float32).reshape(
        row_share, tokens.shape[1]
    )
    own_tokens = lax.dynamic_slice_in_dim(tokens, mlp_index * row_share, row_share)
    residual = (own_tokens.astype(jnp.float32) + dense + delta).astype(jnp.bfloat16)
    normed_two = layer_norm(residual, second_gain)
    expanded = gelu_tanh(
        jnp.dot(
            lax.all_gather(normed_two, "mlp", axis=0, tiled=True),
            up_weight,
            preferred_element_type=jnp.float32,
        )
    ).astype(jnp.bfloat16)
    feed = lax.psum_scatter(
        jnp.dot(expanded, down_weight, preferred_element_type=jnp.float32).astype(jnp.bfloat16),
        "mlp",
        scatter_dimension=0,
        tiled=True,
    ).astype(jnp.float32)
    own_valid = lax.dynamic_slice_in_dim(valid.reshape(-1), mlp_index * row_share, row_share)
    layer_out = jnp.where(
        own_valid[:, None], residual.astype(jnp.float32) + feed, jnp.zeros((), jnp.float32)
    ).astype(jnp.bfloat16)
    flat = fresh.reshape(requests, -1)
    moving = flat[migrants]
    own_slots = req_index * requests + jnp.arange(requests, dtype=jnp.int32)
    lands_here = landing[None, :] == own_slots[:, None]
    arrived = lax.all_gather(moving, "req", axis=0, tiled=True)
    matching = lands_here.astype(jnp.bfloat16)
    picked = jnp.dot(matching, arrived, preferred_element_type=jnp.float32).astype(jnp.bfloat16)
    moved_in = jnp.any(lands_here, axis=1)
    page_out = jnp.where(moved_in[:, None], picked, flat).reshape(
        requests, slot, flat.shape[1] // slot
    )
    return (layer_out, page_out)


def solution(mesh):
    return jax.shard_map(
        shards,
        mesh=mesh,
        in_specs=(
            P("req", None),
            P(),
            P(None, "mlp"),
            P("mlp", None),
            P("req", None, "mlp"),
            P("req", None, None),
            P(),
            P(),
            P(),
            P(None, "mlp"),
            P("mlp", None),
            P("req", None, "mlp"),
            P("req", None),
            P("req"),
            P("req"),
            P("req"),
            P(),
        ),
        out_specs=(P(("req", "mlp"), None), P("req", None, "mlp")),
        check_vma=False,
    )
```

profile of v0, /device:TPU:0, one launch (start us, length us, event | category | flops | bytes accessed | tf_op | source)
XLA Modules:
  0.0 414.1 jit_solution(13141839488661226684)
XLA Ops:
  13.4 3.0 convert_reduce_fusion
  18.1 10.7 %fusion.30 = bf16[1024,1536]{1,0:T(8,128)(2,1)} fusion(bf16[2048,1536]{1,0:T(8,128)(2,1)} %param.19, bf16[1024,2048]{1,0:T(8,128)(2,1)S(1)} %copy-done.4, f32[2048]{0:T(1024)S(1)} %copy-done.12, f32[1024]{0:T(1024)S(1)} %add_rsqrt_fusion, f32[1024]{0:T(1024)S(1)} %broadcast_multiply_fusion.2), kind=kOutput, calls=%fused_computation.39 | convolution fusion | flops 6454509568 | bytes 13647872 | tf_op jit(solution)/shard_map/dot_general | solution.py:86
  28.9 4.6 %copy.112 = bf16[12,128,1024]{1,2,0:T(8,128)(2,1)} copy(bf16[12,128,1024]{2,1,0:T(8,128)(2,1)} %param.28) | data formatting | bytes 6291456 | tf_op args[11]
  33.6 4.6 %copy.115 = bf16[12,128,4,2,128]{4,1,3,2,0:T(8,128)(2,1)} copy(bf16[12,128,4,2,128]{1,4,3,2,0:T(8,128)(2,1)} %bitcast.87) | data formatting | bytes 6291456 | tf_op jit(solution)/shard_map/reshape | solution.py:92
  38.2 6.9 %gather_fusion.1 = bf16[32,128,4,2,128]{4,1,3,2,0:T(8,128)(2,1)} fusion(bf16[12,128,4,2,128]{4,1,3,2,0:T(8,128)(2,1)} %copy.115, s32[1024]{0:T(1024)S(1)} %pad_clamp_fusion.2), kind=kCustom, calls=%fused_computation.1 | custom fusion | bytes 16777344 | tf_op jit(solution)/shard_map/gather | solution.py:93
  45.1 10.4 %copy.116 = bf16[32,128,4,2,128]{4,1,0,3,2:T(8,128)(2,1)} copy(bf16[32,128,4,2,128]{4,1,3,2,0:T(8,128)(2,1)} %gather_fusion.1) | data formatting | bytes 16777216 | tf_op jit(solution)/shard_map/gather | solution.py:93
  55.4 4.7 %copy.118 = bf16[1024,1536]{0,1:T(8,128)(2,1)} copy(bf16[1024,1536]{1,0:T(8,128)(2,1)} %fusion.30) | data formatting | bytes 6291456 | tf_op jit(solution)/shard_map/convert_element_type | solution.py:86
  60.2 2.9 copy.144
  70.7 5.9 %fusion.70 = (bf16[8,512,4,1,128]{4,1,0,3,2:T(8,128)(2,1)}, bf16[8,512,4,1,128]{4,1,0,3,2:T(8,128)(2,1)}) fusion(bf16[8,512,4,2,128]{4,1,0,3,2:T(8,128)(2,1)} %bitcast.83), kind=kLoop, calls=%fused_computation.116 | loop fusion | bytes 16777216 | tf_op jit(solution)/shard_map/slice | solution.py:104
  76.7 6.4 %copy.137 = bf16[8,512,4,1,128]{1,4,2,0,3:T(8,128)(2,1)} copy(bf16[8,512,4,1,128]{4,1,0,3,2:T(8,128)(2,1)} %get-tuple-element.17) | data formatting | bytes 8388608
  90.9 3.5 fusion.18
  100.0 5.6 %convolution_convert_fusion.1 = bf16[1024,2048]{1,0:T(8,128)(2,1)} fusion(bf16[512,2048]{1,0:T(8,128)(2,1)S(1)} %copy-done, bf16[64,8,8,128]{3,2,1,0:T(8,128)(2,1)} %bitcast.93), kind=kOutput, calls=%fused_computation.40 | convolution fusion | flops 2149580800 | bytes 7340032 | tf_op jit(solution)/shard_map/dot_general | solution.py:125
  107.5 3.2 copy.133
  118.0 8.8 %all-gather.8.cloned.1.call-done = bf16[64,16,2048]{2,0,1:T(8,128)(2,1)} async-done(((bf16[8,16,2048]{2,0,1:T(8,128)(2,1)}), bf16[64,16,2048]{2,0,1:T(8,128)(2,1)}) %all-gather.8.cloned.1.call-update) | async-done | bytes 4194320 | tf_op jit(solution)/shard_map/all_gather | solution.py:113
  126.8 2.9 fusion.56
  129.9 17.0 %reduce-scatter.6.cloned.1.call-done = bf16[256,16]{0,1:T(8,128)(2,1)} async-done(((bf16[1024,16]{0,1:T(8,128)(2,1)}), bf16[256,16]{0,1:T(8,128)(2,1)}) %reduce-scatter.6.cloned.1.call-update) | async-done | bytes 8208 | tf_op jit(solution)/shard_map/reduce_scatter | solution.py:138
  148.0 45.9 %reduce-scatter.4.cloned.1.call-done = bf16[256,2048]{1,0:T(8,128)(2,1)} async-done(((bf16[1024,2048]{1,0:T(8,128)(2,1)}), bf16[256,2048]{1,0:T(8,128)(2,1)}) %reduce-scatter.4.cloned.1.call-update) | async-done | bytes 1048592 | tf_op jit(solution)/shard_map/reduce_scatter | solution.py:135
  198.0 2.7 maximum_bitcast_fusion
  200.8 31.8 %all-gather.10.cloned.1.call-done = bf16[1024,2048]{1,0:T(8,128)(2,1)} async-done(((bf16[256,2048]{1,0:T(8,128)(2,1)}), bf16[1024,2048]{1,0:T(8,128)(2,1)}) %all-gather.10.cloned.1.call-update) | async-done | bytes 4194320 | tf_op jit(solution)/shard_map/all_gather | solution.py:152
  232.6 25.4 %fusion.27 = bf16[1024,2048]{1,0:T(8,128)(2,1)} fusion(bf16[2048,2048]{1,0:T(8,128)(2,1)} %param.27, bf16[1024,2048]{1,0:T(8,128)(2,1)} %all-gather.10.cloned.1.call-done, bf16[2048,2048]{1,0:T(8,128)(2,1)} %param.26), kind=kOutput, calls=%fused_computation.38 | convolution fusion | flops 17200840704 | bytes 25165824 | tf_op jit(solution)/shard_map/dot_general | solution.py:158
  258.8 100.7 %all-gather.12.cloned.1.call-done = bf16[8,4,131072]{2,1,0:T(4,128)(2,1)} async-done(((bf16[1,4,131072]{2,1,0:T(4,128)(2,1)}), bf16[8,4,131072]{2,1,0:T(4,128)(2,1)}) %all-gather.12.cloned.1.call-update) | async-done | bytes 8388624 | tf_op jit(solution)/shard_map/all_gather | solution.py:171
  359.5 7.7 %reshape.302 = bf16[32,131072]{1,0:T(8,128)(2,1)} reshape(bf16[8,4,131072]{2,1,0:T(4,128)(2,1)} %all-gather.12.cloned.1.call-done) | data formatting | bytes 16777216
  367.3 6.7 %fusion = bf16[8,131072]{1,0:T(8,128)(2,1)S(1)} fusion(bf16[8,131072]{1,0:T(8,128)(2,1)} %copy-done.5, bf16[32,131072]{1,0:T(8,128)(2,1)} %reshape.302, pred[8]{0:T(512)(128)(4,1)S(1)} %compare_reduce_fusion, s32[32]{0:T(128)S(1)} %copy-done.10, s32[8]{0:T(128)S(1)} %iota_add_fusion), kind=kOutput, calls=%fused_computation.6 | convolution fusion | flops 69206272 | bytes 12583080 | tf_op jit(solution)/shard_map/dot_general | solution.py:173
  376.4 28.3 %reduce-scatter.8.cloned.1.call-done = bf16[256,2048]{1,0:T(8,128)(2,1)} async-done(((bf16[1024,2048]{1,0:T(8,128)(2,1)}), bf16[256,2048]{1,0:T(8,128)(2,1)}) %reduce-scatter.8.cloned.1.call-update) | async-done | bytes 1048592 | tf_op jit(solution)/shard_map/reduce_scatter | solution.py:157
  (104 shorter events, 49.4 us)
Async XLA Ops:
  7.2 92.8 %copy-start = (bf16[512,2048]{1,0:T(8,128)(2,1)S(1)}, bf16[512,2048]{1,0:T(8,128)(2,1)}, u32[]{:S(2)}) copy-start(bf16[512,2048]{1,0:T(8,128)(2,1)} %param.20) | copy-start | bytes 6291460
  7.2 90.3 %all-gather.6.cloned.1.call-start = ((), (), s32[]{:S(2)}) async-start(), calls=%async_computation.4 | async-start | bytes 1179648 | tf_op jit(solution)/shard_map/all_gather | solution.py:112
  9.0 117.8 %all-gather.8.cloned.1.call-start = ((), (), s32[]{:S(2)}) async-start(), calls=%async_computation.6 | async-start | bytes 4718592 | tf_op jit(solution)/shard_map/all_gather | solution.py:113
  11.3 135.6 %reduce-scatter.6.cloned.1.call-start = ((), (), s32[]{:S(2)}) async-start(), calls=%async_computation.5 | async-start | bytes 40960 | tf_op jit(solution)/shard_map/reduce_scatter | solution.py:138
  13.4 3.4 copy-start.4
  13.4 4.7 %copy-start.12 = (f32[2048]{0:T(1024)S(1)}, f32[2048]{0:T(1024)}, u32[]{:S(2)}) copy-start(f32[2048]{0:T(1024)} %param.18) | copy-start | bytes 24580
  63.1 1.7 copy-start.3
  76.7 6.5 %copy-start.11 = (s32[8]{0:T(128)S(1)}, s32[8]{0:T(128)}, u32[]{:S(2)}) copy-start(s32[8]{0:T(128)} %param.31) | copy-start | bytes 100
  83.1 3.3 copy-start.6
  88.3 2.5 copy-start.7
  90.9 3.5 copy-start.8
  94.4 2.5 copy-start.2
  100.0 94.0 %reduce-scatter.4.cloned.1.call-start = ((), (), s32[]{:S(2)}) async-start(), calls=%async_computation.3 | async-start | bytes 5242880 | tf_op jit(solution)/shard_map/reduce_scatter | solution.py:135
  105.6 127.0 %all-gather.10.cloned.1.call-start = ((), (), s32[]{:S(2)}) async-start(), calls=%async_computation.7 | async-start | bytes 5242880 | tf_op jit(solution)/shard_map/all_gather | solution.py:152
  105.6 5.1 %copy-start.13 = (s32[4]{0:T(128)S(1)}, s32[4]{0:T(128)}, u32[]{:S(2)}) copy-start(s32[4]{0:T(128)} %param.32) | copy-start | bytes 52
  112.9 1.3 copy-start.5
  129.9 66.7 %copy-start.9 = (f32[2048]{0:T(1024)S(1)}, f32[2048]{0:T(1024)}, u32[]{:S(2)}) copy-start(f32[2048]{0:T(1024)} %param.25) | copy-start | bytes 24580
  198.0 161.6 %all-gather.12.cloned.1.call-start = ((), (), s32[]{:S(2)}) async-start(), calls=%async_computation.9 | async-start | bytes 9437184 | tf_op jit(solution)/shard_map/all_gather | solution.py:171
  200.7 204.0 %reduce-scatter.8.cloned.1.call-start = ((), (), s32[]{:S(2)}) async-start(), calls=%async_computation.8 | async-start | bytes 5242880 | tf_op jit(solution)/shard_map/reduce_scatter | solution.py:157
  258.0 0.7 copy-start.10
  367.3 40.0 %copy-start.1 = (bf16[512,2048]{1,0:T(8,128)(2,1)S(1)}, bf16[512,2048]{1,0:T(8,128)(2,1)}, u32[]{:S(2)}) copy-start(bf16[512,2048]{1,0:T(8,128)(2,1)} %param.20) | copy-start | bytes 6291460
Sparse Core Ops, SparseCore 0:
  10.1 42.2 all-gather.5
  54.5 72.2 all-gather.7
  129.2 17.6 reduce-scatter.5
  149.4 44.4 reduce-scatter.3
  198.1 34.4 all-gather.9
  234.6 124.9 all-gather.11
  362.0 42.6 reduce-scatter.7
where the time goes:
time: 415 us; the launch traced here: 414 us
  waiting for transfers between devices  233 us (56%)
  local copies, waits for them, and re-layouts  84.5 us (20%)
  matrix products  62.4 us (15%)
  other arithmetic  19.8 us (5%)
  between operations  14.5 us (3%)
    all_gather x1, waiting for transfers between devices, shards(): arrived = lax.all_gather(moving, 'req', axis=0, tiled=True)  101 us
    reduce_scatter x1, waiting for transfers between devices, shards(): lax.psum_scatter(dense_part.astype(jnp.bfloat16), 'mlp', scatter_dimensio...  45.9 us
    unnamed x37, local copies, waits for them, and re-layouts  36.4 us
    all_gather x1, waiting for transfers between devices, shards(): lax.all_gather(normed_two, 'mlp', axis=0, tiled=True)  31.8 us
    reduce_scatter x1, waiting for transfers between devices, shards(): lax.psum_scatter(jnp.dot(expanded, down_weight, preferred_element_type=jn...  28.3 us
    dot_general x1, matrix products, shards(): jnp.dot(expanded, down_weight, preferred_element_type=jnp.float32)  25.4 us
    gather x2, local copies, waits for them, and re-layouts, shards(): pool_view[pages]  17.2 us
    reduce_scatter x1, waiting for transfers between devices, shards(): lax.psum_scatter(low_part.astype(jnp.bfloat16), 'mlp', scatter_dimension=...  17 us
  transfers between devices with their start and end apart: 7, of which 6 were waited for; matrix products, arithmetic and copies ran while one was open for 37% of the time, Pallas kernels for 0%

commit v1 on v0

--- a/solution.py
+++ b/solution.py
@@ -8,6 +8,34 @@
 HD = 128
 ADAPTERS = 64
 EPS = 1e-05
+
+
+def _bring_tails(panel, pos_dim):
+    panel = jnp.moveaxis(panel, 0, pos_dim)
+    w2 = panel.shape
+    r2 = panel.reshape(*w2[:pos_dim], w2[pos_dim] * w2[pos_dim + 1], *w2[pos_dim + 2 :])
+    return r2
+
+
+def review_trees(z, peer_axis, axis_k):
+    world_n = lax.axis_size(peer_axis)
+    in_order = list(map(lambda to_i: (to_i, (to_i + 1) % world_n), range(world_n)))
+    series = [(tick, t) for t, tick in in_order]
+    x_now, d_next = ([], [])
+    for idx in range(world_n - 1):
+        if idx % 2 == 0:
+            x_now.append(
+                lax.ppermute(x_now[-1] if x_now else z, perm=in_order, axis_name=peer_axis)
+            )
+        else:
+            d_next.append(
+                lax.ppermute(d_next[-1] if d_next else z, axis_name=peer_axis, perm=series)
+            )
+    kept_arr = jnp.stack([*x_now[::-1], z, *d_next], 0)
+    carry_out = lax.axis_index(peer_axis) - len(x_now)
+    kept_arr = kept_arr[(jnp.arange(world_n) - carry_out) % world_n]
+    u_next = _bring_tails(kept_arr, axis_k)
+    return u_next
 
 
 def layer_norm(values, gain):
@@ -148,11 +176,7 @@
     residual = (own_tokens.astype(jnp.float32) + dense + delta).astype(jnp.bfloat16)
     normed_two = layer_norm(residual, second_gain)
     expanded = gelu_tanh(
-        jnp.dot(
-            lax.all_gather(normed_two, "mlp", axis=0, tiled=True),
-            up_weight,
-            preferred_element_type=jnp.float32,
-        )
+        jnp.dot(review_trees(normed_two, "mlp", 0), up_weight, preferred_element_type=jnp.float32)
     ).astype(jnp.bfloat16)
     feed = lax.psum_scatter(
         jnp.dot(expanded, down_weight, preferred_element_type=jnp.float32).astype(jnp.bfloat16),

time: 415 us -> 380 us (0.916)
  waiting for transfers between devices: 233 us -> 186 us
    all_gather x1, waiting for transfers between devices: 101 us -> 48.9 us  [shards(): arrived = lax.all_gather(moving, 'req', axis=0, tiled=True)]
    ppermute x0 -> x3, waiting for transfers between devices: none -> 37.4 us  [the longest x2 37.4 us: review_trees(): lax.ppermute(x_now[-1] if x_now else z, perm=in_order, axis_name=peer_axis)]
    all_gather x1 -> x0, waiting for transfers between devices: 31.8 us -> none  [shards(): lax.all_gather(normed_two, 'mlp', axis=0, tiled=True)]
    gather x0 -> x1, local copies, waits for them, and re-layouts: none -> 4.94 us  [review_trees(): kept_arr = kept_arr[(jnp.arange(world_n) - carry_out) % world_n]]
  transfers between devices with their start and end apart: 7 -> 9, of which waited for: 6 -> 7; matrix products, arithmetic and copies ran while one was open for 37% -> 44% of each run, Pallas kernels for 0% -> 0%
where the time goes in v1:
time: 380 us; the launch traced here: 376 us
  waiting for transfers between devices  186 us (49%)
  local copies, waits for them, and re-layouts  87.9 us (23%)
  matrix products  63.7 us (17%)
  other arithmetic  21.7 us (6%)
  between operations  14.7 us (4%)
    all_gather x1, waiting for transfers between devices, shards(): arrived = lax.all_gather(moving, 'req', axis=0, tiled=True)  48.9 us
    reduce_scatter x1, waiting for transfers between devices, shards(): lax.psum_scatter(dense_part.astype(jnp.bfloat16), 'mlp', scatter_dimensio...  45.9 us
    ppermute x2, waiting for transfers between devices, review_trees(): lax.ppermute(x_now[-1] if x_now else z, perm=in_order, axis_name=peer_axis)  37.4 us
    unnamed x37, local copies, waits for them, and re-layouts  36.3 us
    reduce_scatter x1, waiting for transfers between devices, shards(): lax.psum_scatter(jnp.dot(expanded, down_weight, preferred_element_type=jn...  28.3 us
    dot_general x1, matrix products, shards(): jnp.dot(expanded, down_weight, preferred_element_type=jnp.float32)  26.5 us
    gather x2, local copies, waits for them, and re-layouts, shards(): pool_view[pages]  17.2 us
    reduce_scatter x1, waiting for transfers between devices, shards(): lax.psum_scatter(low_part.astype(jnp.bfloat16), 'mlp', scatter_dimension=...  17 us
  transfers between devices with their start and end apart: 9, of which 7 were waited for; matrix products, arithmetic and copies ran while one was open for 44% of the time, Pallas kernels for 0%

profile of v1, /device:TPU:0, one launch (start us, length us, event | category | flops | bytes accessed | tf_op | source)
XLA Modules:
  0.0 376.1 jit_solution(2110495141836077701)
XLA Ops:
  13.4 3.0 convert_reduce_fusion
  18.1 11.0 %fusion.30 = bf16[1024,1536]{1,0:T(8,128)(2,1)} fusion(bf16[2048,1536]{1,0:T(8,128)(2,1)} %param.19, bf16[1024,2048]{1,0:T(8,128)(2,1)S(1)} %copy-done.4, f32[2048]{0:T(1024)S(1)} %copy-done.12, f32[1024]{0:T(1024)S(1)} %add_rsqrt_fusion, f32[1024]{0:T(1024)S(1)} %broadcast_multiply_fusion.2), kind=kOutput, calls=%fused_computation.41 | convolution fusion | flops 6454509568 | bytes 13647872 | tf_op jit(solution)/shard_map/dot_general | solution.py:114
  29.2 4.6 %copy.112 = bf16[12,128,1024]{1,2,0:T(8,128)(2,1)} copy(bf16[12,128,1024]{2,1,0:T(8,128)(2,1)} %param.28) | data formatting | bytes 6291456 | tf_op args[11]
  33.9 4.6 %copy.115 = bf16[12,128,4,2,128]{4,1,3,2,0:T(8,128)(2,1)} copy(bf16[12,128,4,2,128]{1,4,3,2,0:T(8,128)(2,1)} %bitcast.95) | data formatting | bytes 6291456 | tf_op jit(solution)/shard_map/reshape | solution.py:120
  38.5 6.9 %gather_fusion.1 = bf16[32,128,4,2,128]{4,1,3,2,0:T(8,128)(2,1)} fusion(bf16[12,128,4,2,128]{4,1,3,2,0:T(8,128)(2,1)} %copy.115, s32[1024]{0:T(1024)S(1)} %pad_clamp_fusion.3), kind=kCustom, calls=%fused_computation.1 | custom fusion | bytes 16777344 | tf_op jit(solution)/shard_map/gather | solution.py:121
  45.4 10.4 %copy.116 = bf16[32,128,4,2,128]{4,1,0,3,2:T(8,128)(2,1)} copy(bf16[32,128,4,2,128]{4,1,3,2,0:T(8,128)(2,1)} %gather_fusion.1) | data formatting | bytes 16777216 | tf_op jit(solution)/shard_map/gather | solution.py:121
  55.8 4.7 %copy.118 = bf16[1024,1536]{0,1:T(8,128)(2,1)} copy(bf16[1024,1536]{1,0:T(8,128)(2,1)} %fusion.30) | data formatting | bytes 6291456 | tf_op jit(solution)/shard_map/convert_element_type | solution.py:114
  71.0 5.9 %fusion.72 = (bf16[8,512,4,1,128]{4,1,0,3,2:T(8,128)(2,1)}, bf16[8,512,4,1,128]{4,1,0,3,2:T(8,128)(2,1)}) fusion(bf16[8,512,4,2,128]{4,1,0,3,2:T(8,128)(2,1)} %bitcast.91), kind=kLoop, calls=%fused_computation.125 | loop fusion | bytes 16777216 | tf_op jit(solution)/shard_map/slice | solution.py:132
  76.9 6.4 %copy.137 = bf16[8,512,4,1,128]{1,4,2,0,3:T(8,128)(2,1)} copy(bf16[8,512,4,1,128]{4,1,0,3,2:T(8,128)(2,1)} %get-tuple-element.17) | data formatting | bytes 8388608
  91.1 3.5 fusion.18
  100.3 5.6 %convolution_convert_fusion.1 = bf16[1024,2048]{1,0:T(8,128)(2,1)} fusion(bf16[512,2048]{1,0:T(8,128)(2,1)S(1)} %copy-done, bf16[64,8,8,128]{3,2,1,0:T(8,128)(2,1)} %bitcast.102), kind=kOutput, calls=%fused_computation.42 | convolution fusion | flops 2149580800 | bytes 7340032 | tf_op jit(solution)/shard_map/dot_general | solution.py:153
  107.8 3.2 copy.133
  118.3 8.5 %all-gather.7.cloned.1.call-done = bf16[64,16,2048]{2,0,1:T(8,128)(2,1)} async-done(((bf16[8,16,2048]{2,0,1:T(8,128)(2,1)}), bf16[64,16,2048]{2,0,1:T(8,128)(2,1)}) %all-gather.7.cloned.1.call-update) | async-done | bytes 4194320 | tf_op jit(solution)/shard_map/all_gather | solution.py:141
  129.9 17.0 %reduce-scatter.6.cloned.1.call-done = bf16[256,16]{0,1:T(8,128)(2,1)} async-done(((bf16[1024,16]{0,1:T(8,128)(2,1)}), bf16[256,16]{0,1:T(8,128)(2,1)}) %reduce-scatter.6.cloned.1.call-update) | async-done | bytes 8208 | tf_op jit(solution)/shard_map/reduce_scatter | solution.py:166
  148.0 45.9 %reduce-scatter.4.cloned.1.call-done = bf16[256,2048]{1,0:T(8,128)(2,1)} async-done(((bf16[1024,2048]{1,0:T(8,128)(2,1)}), bf16[256,2048]{1,0:T(8,128)(2,1)}) %reduce-scatter.4.cloned.1.call-update) | async-done | bytes 1048592 | tf_op jit(solution)/shard_map/reduce_scatter | solution.py:163
  198.8 23.2 %collective-permute-done = bf16[256,2048]{1,0:T(8,128)(2,1)} collective-permute-done((bf16[256,2048]{1,0:T(8,128)(2,1)S(1)}, bf16[256,2048]{1,0:T(8,128)(2,1)}, u32[]{:S(2)}, u32[]{:S(2)}) %collective-permute-start) | collective-permute-done | bytes 1048608 | tf_op jit(solution)/shard_map/ppermute | solution.py:28
  222.5 14.1 %collective-permute-done.1 = bf16[256,2048]{1,0:T(8,128)(2,1)} collective-permute-done((bf16[256,2048]{1,0:T(8,128)(2,1)}, bf16[256,2048]{1,0:T(8,128)(2,1)}, u32[]{:S(2)}, u32[]{:S(2)}) %collective-permute-start.1) | collective-permute-done | bytes 1048608 | tf_op jit(solution)/shard_map/ppermute | solution.py:28
  236.6 3.8 pad_maximum_fusion
  240.3 4.9 %gather_fusion.3 = bf16[4,256,2048]{2,1,0:T(8,128)(2,1)} fusion(bf16[4,256,2048]{2,1,0:T(8,128)(2,1)} %pad_maximum_fusion, s32[1024]{0:T(1024)S(1)} %pad_clamp_fusion.1), kind=kCustom, calls=%fused_computation.3 | custom fusion | bytes 8388624 | tf_op jit(solution)/shard_map/gather | solution.py:36
  245.3 26.5 %fusion.27 = bf16[1024,2048]{1,0:T(8,128)(2,1)} fusion(bf16[2048,2048]{1,0:T(8,128)(2,1)} %param.27, bf16[1024,2048]{1,0:T(8,128)(2,1)} %bitcast.99, bf16[2048,2048]{1,0:T(8,128)(2,1)} %param.26), kind=kOutput, calls=%fused_computation.40 | convolution fusion | flops 17200840704 | bytes 25165824 | tf_op jit(solution)/shard_map/dot_general | solution.py:182
  272.6 48.9 %all-gather.9.cloned.1.call-done = bf16[8,4,131072]{2,1,0:T(4,128)(2,1)} async-done(((bf16[1,4,131072]{2,1,0:T(4,128)(2,1)}), bf16[8,4,131072]{2,1,0:T(4,128)(2,1)}) %all-gather.9.cloned.1.call-update) | async-done | bytes 8388624 | tf_op jit(solution)/shard_map/all_gather | solution.py:195
  321.4 7.7 %reshape.363 = bf16[32,131072]{1,0:T(8,128)(2,1)} reshape(bf16[8,4,131072]{2,1,0:T(4,128)(2,1)} %all-gather.9.cloned.1.call-done) | data formatting | bytes 16777216
  329.2 6.6 %fusion = bf16[8,131072]{1,0:T(8,128)(2,1)S(1)} fusion(bf16[8,131072]{1,0:T(8,128)(2,1)} %copy-done.5, bf16[32,131072]{1,0:T(8,128)(2,1)} %reshape.363, pred[8]{0:T(512)(128)(4,1)S(1)} %compare_reduce_fusion, s32[32]{0:T(128)S(1)} %copy-done.10, s32[8]{0:T(128)S(1)} %iota_add_fusion), kind=kOutput, calls=%fused_computation.7 | convolution fusion | flops 69206272 | bytes 12583080 | tf_op jit(solution)/shard_map/dot_general | solution.py:197
  338.2 28.3 %reduce-scatter.8.cloned.1.call-done = bf16[256,2048]{1,0:T(8,128)(2,1)} async-done(((bf16[1024,2048]{1,0:T(8,128)(2,1)}), bf16[256,2048]{1,0:T(8,128)(2,1)}) %reduce-scatter.8.cloned.1.call-update) | async-done | bytes 1048592 | tf_op jit(solution)/shard_map/reduce_scatter | solution.py:181
  (112 shorter events, 56.2 us)
Async XLA Ops:
  7.2 93.1 %copy-start = (bf16[512,2048]{1,0:T(8,128)(2,1)S(1)}, bf16[512,2048]{1,0:T(8,128)(2,1)}, u32[]{:S(2)}) copy-start(bf16[512,2048]{1,0:T(8,128)(2,1)} %param.20) | copy-start | bytes 6291460
  7.2 90.6 %all-gather.5.cloned.1.call-start = ((), (), s32[]{:S(2)}) async-start(), calls=%async_computation.4 | async-start | bytes 1179648 | tf_op jit(solution)/shard_map/all_gather | solution.py:140
  9.0 117.8 %all-gather.7.cloned.1.call-start = ((), (), s32[]{:S(2)}) async-start(), calls=%async_computation.6 | async-start | bytes 4718592 | tf_op jit(solution)/shard_map/all_gather | solution.py:141
  11.3 135.6 %reduce-scatter.6.cloned.1.call-start = ((), (), s32[]{:S(2)}) async-start(), calls=%async_computation.5 | async-start | bytes 40960 | tf_op jit(solution)/shard_map/reduce_scatter | solution.py:166
  13.4 3.4 copy-start.4
  13.4 4.7 %copy-start.12 = (f32[2048]{0:T(1024)S(1)}, f32[2048]{0:T(1024)}, u32[]{:S(2)}) copy-start(f32[2048]{0:T(1024)} %param.18) | copy-start | bytes 24580
  63.4 1.7 copy-start.3
  76.9 6.5 %copy-start.11 = (s32[8]{0:T(128)S(1)}, s32[8]{0:T(128)}, u32[]{:S(2)}) copy-start(s32[8]{0:T(128)} %param.31) | copy-start | bytes 100
  83.4 3.3 copy-start.6
  88.6 2.5 copy-start.7
  91.1 3.5 copy-start.8
  94.6 2.5 copy-start.2
  100.2 93.7 %reduce-scatter.4.cloned.1.call-start = ((), (), s32[]{:S(2)}) async-start(), calls=%async_computation.3 | async-start | bytes 5242880 | tf_op jit(solution)/shard_map/reduce_scatter | solution.py:163
  105.9 215.6 %all-gather.9.cloned.1.call-start = ((), (), s32[]{:S(2)}) async-start(), calls=%async_computation.8 | async-start | bytes 9437184 | tf_op jit(solution)/shard_map/all_gather | solution.py:195
  111.4 3.3 copy-start.13
  113.2 1.3 copy-start.5
  118.3 248.3 %reduce-scatter.8.cloned.1.call-start = ((), (), s32[]{:S(2)}) async-start(), calls=%async_computation.7 | async-start | bytes 5242880 | tf_op jit(solution)/shard_map/reduce_scatter | solution.py:181
  129.9 66.7 %copy-start.9 = (f32[2048]{0:T(1024)S(1)}, f32[2048]{0:T(1024)}, u32[]{:S(2)}) copy-start(f32[2048]{0:T(1024)} %param.25) | copy-start | bytes 24580
  197.0 25.0 %collective-permute-start = (bf16[256,2048]{1,0:T(8,128)(2,1)S(1)}, bf16[256,2048]{1,0:T(8,128)(2,1)}, u32[]{:S(2)}, u32[]{:S(2)}) collective-permute-start(bf16[256,2048]{1,0:T(8,128)(2,1)S(1)} %fusion.37), channel_id=1, source_target_pairs={{0,1},{1,2},{2,3},{3,0},{4,5},{5,6},{6,7},{7,4},{8,9},{9,10},{10,1... | collective-permute-start | bytes 3145736 | tf_op jit(solution)/shard_map/ppermute | solution.py:28
  197.0 25.4 %collective-permute-start.2 = (bf16[256,2048]{1,0:T(8,128)(2,1)S(1)}, bf16[256,2048]{1,0:T(8,128)(2,1)}, u32[]{:S(2)}, u32[]{:S(2)}) collective-permute-start(bf16[256,2048]{1,0:T(8,128)(2,1)S(1)} %fusion.37), channel_id=1, source_target_pairs={{1,0},{2,1},{3,2},{0,3},{5,4},{6,5},{7,6},{4,7},{9,8},{10,9},{11,1... | collective-permute-start | bytes 3145736 | tf_op jit(solution)/shard_map/ppermute | solution.py:32
  222.0 14.5 %collective-permute-start.1 = (bf16[256,2048]{1,0:T(8,128)(2,1)}, bf16[256,2048]{1,0:T(8,128)(2,1)}, u32[]{:S(2)}, u32[]{:S(2)}) collective-permute-start(bf16[256,2048]{1,0:T(8,128)(2,1)} %collective-permute-done), channel_id=1, source_target_pairs={{0,1},{1,2},{2,3},{3,0},{4,5},{5,6},{6,7},{7,4},{8,9},{9,10},{10,1... | collective-permute-start | bytes 3145736 | tf_op jit(solution)/shard_map/ppermute | solution.py:28
  271.7 0.7 copy-start.10
  329.2 39.9 %copy-start.1 = (bf16[512,2048]{1,0:T(8,128)(2,1)S(1)}, bf16[512,2048]{1,0:T(8,128)(2,1)}, u32[]{:S(2)}) copy-start(bf16[512,2048]{1,0:T(8,128)(2,1)} %param.20) | copy-start | bytes 6291460
Sparse Core Ops, SparseCore 0:
  10.1 42.2 all-gather.4
  54.5 72.2 all-gather.6
  129.2 17.6 reduce-scatter.5
  149.4 44.4 reduce-scatter.3
  196.5 124.9 all-gather.8
  323.8 42.6 reduce-scatter.7
